TPU v7x, 128 devices: a whole 4x4x4 slice. The times are simulated.
128 devices in a mesh: ctx: 16 (over x, y_lo, core), ch: 8 (over y_hi, z).
Axes of the slice: x: 4, y: 4 (y_hi: 2, y_lo: 2; y = y_hi * 2 + y_lo), z: 4, core: 2. Of those that a mesh axis runs over, the one named last changes fastest.
Arguments:
- query_in: bfloat16 [3072, 8192], P('ctx', 'ch'), may hold values from -6 to 6
- key_in: bfloat16 [3072, 8192], P('ctx', 'ch'), may hold values from -6 to 6
- value_in: bfloat16 [3072, 8192], P('ctx', 'ch'), may hold values from -6 to 6
- filters: bfloat16 [512, 3072], P('ch'), may hold values from -0.8 to 0.8
- skip_gain: float32 [8192], P('ch'), may hold values from -3 to 3
- out_weight: bfloat16 [8192, 8192], P(None, 'ch'), may hold values from -0.0625 to 0.0625
Outputs:
- output: bfloat16 [3072, 8192], P('ctx', 'ch')
All inputs are finite; a program needn't handle non-finite values.
Results may differ from a plain program's by a relative error of at most 0.0057.
Values may be sent and summed in bfloat16 or wider, within the bound.
No kernel may reach another device: no remote copies, remote signals or barrier semaphores. Data moves between devices by JAX's collectives and lax.ppermute only.
A program may use at most 128 MiB of HBM per device.

v0:
```python
import jax
import jax.numpy as jnp
from jax import lax
from jax.sharding import PartitionSpec as P


def toeplitz(padded, offset, out_rows, src_rows):
    groups = padded.shape[0]
    seq_len = padded.shape[1] // 2
    width = out_rows + src_rows - 1
    segment = lax.dynamic_slice_in_dim(padded, offset - src_rows + 1 + seq_len, width, 1)
    flipped = jnp.concatenate([segment[:, ::-1], jnp.zeros((groups, 1), segment.dtype)], axis=1)
    period = width + 1
    repeated = jnp.broadcast_to(flipped[:, None, :], (groups, out_rows, period)).reshape(
        groups, out_rows * period
    )
    sheared = repeated[:, out_rows - 1 : out_rows - 1 + out_rows * width].reshape(
        groups, out_rows, width
    )
    return sheared[:, :, :src_rows]


def conv_term(padded, offset, out_rows, source):
    tiles = toeplitz(padded, offset, out_rows, source.shape[0])
    grouped = source.reshape(source.shape[0], padded.shape[0], -1)
    result = jnp.einsum("grs,sgc->rgc", tiles, grouped, preferred_element_type=jnp.float32)
    return result.reshape(out_rows, -1)


def causal_add(summed, padded, out_start, out_rows, source, src_start):

    def include(current):
        return current + conv_term(padded, out_start - src_start, out_rows, source)

    def leave(current):
        return current

    return lax.cond(src_start < out_start + out_rows, include, leave, summed)


def apply_gate(query_part, conv, gain, mixed_part):
    total = conv + gain[None, :] * mixed_part.astype(jnp.float32)
    return (query_part.astype(jnp.float32) * total).astype(jnp.bfloat16)


def project(gated, out_weight):
    total = jnp.dot(
        lax.all_gather(gated, "ch", axis=1, tiled=True),
        out_weight,
        preferred_element_type=jnp.float32,
    )
    return total.astype(jnp.bfloat16)


def shards(query_in, key_in, value_in, filters, skip_gain, out_weight):
    block_rows = query_in.shape[0]
    channels = query_in.shape[1]
    cycle_pos = lax.axis_index("ctx")
    mixed = (key_in.astype(jnp.float32) * value_in.astype(jnp.float32)).astype(jnp.bfloat16)
    padded = jnp.concatenate([jnp.zeros_like(filters), filters], axis=1)
    out_start = cycle_pos * block_rows
    empty = jnp.zeros((block_rows, channels), jnp.float32)
    portion = lax.all_gather(mixed, "ctx", axis=0, tiled=True)
    height = portion.shape[0]
    pieces = portion.reshape(height // block_rows, block_rows, channels)

    def advance(running, element):
        position, piece = element
        return (
            causal_add(running, padded, out_start, block_rows, piece, position * block_rows),
            None,
        )

    running, _ = lax.scan(
        advance, empty, (jnp.arange(height // block_rows, dtype=jnp.int32), pieces)
    )
    return project(apply_gate(query_in, running, skip_gain, mixed), out_weight)


def solution(mesh):
    placed = (P("ctx", "ch"), P("ctx", "ch"), P("ctx", "ch"), P("ch", None), P("ch"), P(None, "ch"))
    return jax.shard_map(
        shards, mesh=mesh, in_specs=placed, out_specs=P("ctx", "ch"), check_vma=False
    )
```

profile of v0, /device:TPU:0, one launch (start us, length us, event | category | flops | bytes accessed | tf_op | source)
XLA Modules:
  0.0 1123.3 jit_solution(5549705480522828979)
XLA Ops:
  6.5 0.0 all-gather.3.cloned.1.call-start
  6.5 2.0 multiply_convert_fusion.1
  8.5 0.0 all-gather.3.cloned.1.call-update
  8.6 0.0 all-gather.5.cloned.1.call-start
  8.6 1.1 concatenate.6
  9.7 44.2 %all-gather.3.cloned.1.call-done = bf16[3072,1024]{1,0:T(8,128)(2,1)} async-done(((bf16[192,1024]{1,0:T(8,128)(2,1)}), bf16[3072,1024]{1,0:T(8,128)(2,1)}) %all-gather.3.cloned.1.call-update) | async-done | bytes 6291472 | tf_op jit(solution)/shard_map/all_gather | solution.py:63
  53.9 11.0 copy.11
  64.9 0.1 broadcast_in_dim.5
  65.0 0.0 copy-start
  65.0 0.0 copy-start.1
  65.0 0.0 copy-start.2
  65.0 81.9 %while.14 = (s32[]{:T(128)}, f32[192,1024]{0,1:T(8,128)S(1)}, s32[16]{0:T(128)S(1)}, s32[]{:T(128)}, s32[]{:T(128)}, /*index=5*/bf16[64,6144]{1,0:T(8,128)(2,1)S...) while((s32[]{:T(128)}, f32[192,1024]{0,1:T(8,128)S(1)}, s32[16]{0:T(128)S(1)}, s32[]{:T(128)}, ...), condition=%wide.region_3.4_spmd, body=%wide.region_0.3_spmd.sunk | while | flops 75694096 | bytes 77020792 | solution.py:74
  65.0 0.7 dynamic_slice.19
  66.4 59.7 %conditional.2 = (f32[192,1024]{0,1:T(8,128)S(1)}) conditional(s32[]{:T(128)} %convert_element_type.40, f32[192,1024]{0,1:T(8,128)S(1)} %get-tuple-element.186, (s32[]{:T(128)}, s32[]{:T(128)}, bf16[64,6144]{1,0:T(8,128)(2,1)S(1)}, bf16[16,192,1024]{1,2,0:T(8,128)(2,1)}, s32[]{:T(128)}, /*index=5*/f32[192,1024]{0,1:T(8,128)S(1)}) %tuple.35), branch_computations={%region_1.1_spmd, %region_2.2_spmd} | conditional | flops 75694088 | bytes 77020616 | solution.py:38
  66.4 0.1 constant_dynamic-slice_fusion.1
  66.5 0.3 reverse
  66.7 0.1 slice.12
  66.9 4.5 broadcast_in_dim.1
  71.3 13.3 %copy.13 = bf16[8,8,192,384]{3,1,2,0:T(8,128)(2,1)} copy(bf16[8,8,192,384]{3,2,1,0:T(8,128)(2,1)} %bitcast.15) | data formatting | bytes 18874368 | tf_op jit(solution)/shard_map/while/body/eval_jaxpr/cond
  84.7 9.8 slice.8
  94.5 25.7 %reshape.21 = bf16[64,192,383]{2,1,0:T(8,128)(2,1)} reshape(bf16[64,73536]{1,0:T(8,128)(2,1)} %slice.8) | data formatting | bytes 18825216 | tf_op jit(solution)/shard_map/while/body/eval_jaxpr/cond/branch_1_fun/reshape | solution.py:17
  120.2 1.1 constant_dynamic-slice_fusion
  121.3 4.5 fusion
  125.8 0.2 bitcast_add_fusion
  126.1 0.7 dynamic_slice.19
  127.4 0.7 dynamic_slice.19
  128.8 0.7 dynamic_slice.19
  130.2 0.7 dynamic_slice.19
  131.6 0.7 dynamic_slice.19
  132.9 0.7 dynamic_slice.19
  134.3 0.7 dynamic_slice.19
  135.7 0.7 dynamic_slice.19
  137.1 0.7 dynamic_slice.19
  138.4 0.7 dynamic_slice.19
  139.8 0.7 dynamic_slice.19
  141.2 0.7 dynamic_slice.19
  142.6 0.7 dynamic_slice.19
  143.9 0.7 dynamic_slice.19
  145.3 0.7 dynamic_slice.19
  146.9 0.3 copy.12
  147.2 0.0 copy-done
  147.2 0.0 copy-done.1
  147.2 0.0 copy-done.2
  147.2 0.9 multiply_convert_fusion
  148.1 0.0 all-gather.5.cloned.1.call-update
  148.2 957.4 %all-gather.5.cloned.1.call-done = bf16[192,8192]{1,0:T(8,128)(2,1)} async-done(((bf16[192,1024]{1,0:T(8,128)(2,1)}), bf16[192,8192]{1,0:T(8,128)(2,1)}) %all-gather.5.cloned.1.call-update) | async-done | bytes 3145744 | tf_op jit(solution)/shard_map/all_gather | solution.py:48
  1105.6 10.9 convolution_convert_fusion
  (17 shorter events, 0.2 us)
Async XLA Ops:
  6.5 47.3 %all-gather.3.cloned.1.call-start = ((), (), s32[]{:S(2)}) async-start(), calls=%async_computation | async-start | bytes 6684672 | tf_op jit(solution)/shard_map/all_gather | solution.py:63
  8.6 1097.0 %all-gather.5.cloned.1.call-start = ((), (), s32[]{:S(2)}) async-start(), calls=%async_computation.1 | async-start | bytes 3538944 | tf_op jit(solution)/shard_map/all_gather | solution.py:48
  65.0 82.2 %copy-start = (bf16[192,1024]{1,0:T(8,128)(2,1)S(1)}, bf16[192,1024]{1,0:T(8,128)(2,1)}, u32[]{:S(2)}) copy-start(bf16[192,1024]{1,0:T(8,128)(2,1)} %multiply_convert_fusion.1) | copy-start | bytes 1179652
  65.0 82.2 %copy-start.1 = (bf16[192,1024]{1,0:T(8,128)(2,1)S(1)}, bf16[192,1024]{1,0:T(8,128)(2,1)}, u32[]{:S(2)}) copy-start(bf16[192,1024]{1,0:T(8,128)(2,1)} %param.10) | copy-start | bytes 1179652
  65.0 82.2 %copy-start.2 = (f32[1024]{0:T(1024)S(1)}, f32[1024]{0:T(1024)}, u32[]{:S(2)}) copy-start(f32[1024]{0:T(1024)} %param.14) | copy-start | bytes 12292
Sparse Core Ops, SparseCore 0:
  9.0 44.7 all-gather.2
  148.3 957.2 all-gather.4
where the time goes:
time: 1130 us; the launch traced here: 1120 us
  waiting for transfers between devices  1000 us (88%)
  local copies, waits for them, and re-layouts  77.8 us (7%)
  matrix products  15.4 us (1%)
  between operations  13.5 us (1%)
  loops' own time  11.8 us (1%)
    all_gather x1, waiting for transfers between devices, project(): lax.all_gather(gated, 'ch', axis=1, tiled=True)  957 us
    all_gather x1, waiting for transfers between devices, shards(): portion = lax.all_gather(mixed, 'ctx', axis=0, tiled=True)  44.2 us
    reshape x1, local copies, waits for them, and re-layouts, toeplitz(): repeated[:, out_rows - 1:out_rows - 1 + out_rows * width]  25.7 us
  transfers between devices with their start and end apart: 2, of which 2 were waited for; matrix products, arithmetic and copies ran while one was open for 0% of the time, Pallas kernels for 0%

commit v1 on v0

--- a/solution.py
+++ b/solution.py
@@ -2,6 +2,13 @@
 import jax.numpy as jnp
 from jax import lax
 from jax.sharding import PartitionSpec as P
+
+
+def exchange_gather(x, mesh_axis, dim):
+    devices = lax.axis_size(mesh_axis)
+    shards = jnp.stack([x for _ in range(devices)])
+    shards = lax.all_to_all(shards, mesh_axis, split_axis=0, concat_axis=0)
+    return jnp.concatenate(shards, axis=dim)
 
 
 def toeplitz(padded, offset, out_rows, src_rows):
@@ -44,11 +51,7 @@
 
 
 def project(gated, out_weight):
-    total = jnp.dot(
-        lax.all_gather(gated, "ch", axis=1, tiled=True),
-        out_weight,
-        preferred_element_type=jnp.float32,
-    )
+    total = jnp.dot(exchange_gather(gated, "ch", 1), out_weight, preferred_element_type=jnp.float32)
     return total.astype(jnp.bfloat16)
 
 

time: 1130 us -> 1080 us (0.956)
  the two profiles are of different devices: /device:TPU:0 before, /device:TPU:15 now
where the time goes in v1:
time: 1080 us
  local copies, waits for them, and re-layouts  901 us (83%)
  matrix products  76.3 us (7%)
  waiting for transfers between devices  43.5 us (4%)
  blocking collectives  28.8 us (3%)
  between operations  13.5 us (1%)
  loops' own time  11.4 us (1%)
    reshape x16, local copies, waits for them, and re-layouts, toeplitz(): repeated[:, out_rows - 1:out_rows - 1 + out_rows * width]  412 us
    cond x48, local copies, waits for them, and re-layouts  219 us
    slice x16, local copies, waits for them, and re-layouts, toeplitz(): repeated[:, out_rows - 1:out_rows - 1 + out_rows * width]  157 us
    dot_general x16, matrix products, conv_term(): jnp.einsum('grs,sgc->rgc', tiles, grouped, preferred_element_type=jnp.flo...  72 us
    broadcast_in_dim x16, local copies, waits for them, and re-layouts, toeplitz(): jnp.broadcast_to(flipped[:, None, :], (groups, out_rows, period))  71.6 us
    all_gather x1, waiting for transfers between devices, shards(): portion = lax.all_gather(mixed, 'ctx', axis=0, tiled=True)  43.5 us
    all_to_all x1, blocking collectives, exchange_gather(): shards = lax.all_to_all(shards, mesh_axis, split_axis=0, concat_axis=0)  28.8 us
    dynamic_slice x32, local copies, waits for them, and re-layouts, shards(): lax.scan(advance, empty, (jnp.arange(height // block_rows, dtype=jnp.int3...  26.7 us
  transfers between devices with their start and end apart: 1, of which 1 were waited for; matrix products, arithmetic and copies ran while one was open for 0% of the time, Pallas kernels for 0%

profile of v1, /device:TPU:15, one launch (start us, length us, event | category | flops | bytes accessed | tf_op | source)
XLA Modules:
  0.0 1080.6 jit_solution(12584799485360475080)
XLA Ops:
  9.6 43.5 %all-gather.2.cloned.1.call-done = bf16[3072,1024]{1,0:T(8,128)(2,1)} async-done(((bf16[192,1024]{1,0:T(8,128)(2,1)}), bf16[3072,1024]{1,0:T(8,128)(2,1)}) %all-gather.2.cloned.1.call-update) | async-done | bytes 6291472 | tf_op jit(solution)/shard_map/all_gather | solution.py:66
  64.3 975.0 %while.14 = (s32[]{:T(128)}, f32[192,1024]{0,1:T(8,128)S(1)}, s32[16]{0:T(128)S(1)}, s32[]{:T(128)}, s32[]{:T(128)}, /*index=5*/bf16[64,6144]{1,0:T(8,128)(2,1)S...) while((s32[]{:T(128)}, f32[192,1024]{0,1:T(8,128)S(1)}, s32[16]{0:T(128)S(1)}, s32[]{:T(128)}, ...), condition=%wide.region_3.4_spmd, body=%wide.region_0.3_spmd.sunk | while | flops 75694096 | bytes 77020792 | solution.py:77
  65.5 59.7 %conditional.2 = (f32[192,1024]{0,1:T(8,128)S(1)}) conditional(s32[]{:T(128)} %convert_element_type.40, f32[192,1024]{0,1:T(8,128)S(1)} %get-tuple-element.193, (s32[]{:T(128)}, s32[]{:T(128)}, bf16[64,6144]{1,0:T(8,128)(2,1)S(1)}, bf16[16,192,1024]{1,2,0:T(8,128)(2,1)}, s32[]{:T(128)}, /*index=5*/f32[192,1024]{0,1:T(8,128)S(1)}) %tuple.36), branch_computations={%region_1.1_spmd, %region_2.2_spmd} | conditional | flops 75694088 | bytes 77020616 | solution.py:45
  70.5 13.3 %copy.17 = bf16[8,8,192,384]{3,1,2,0:T(8,128)(2,1)} copy(bf16[8,8,192,384]{3,2,1,0:T(8,128)(2,1)} %bitcast.18) | data formatting | bytes 18874368 | tf_op jit(solution)/shard_map/while/body/eval_jaxpr/cond
  93.7 25.7 %reshape.27 = bf16[64,192,383]{2,1,0:T(8,128)(2,1)} reshape(bf16[64,73536]{1,0:T(8,128)(2,1)} %slice.8) | data formatting | bytes 18825216 | tf_op jit(solution)/shard_map/while/body/eval_jaxpr/cond/branch_1_fun/reshape | solution.py:24
  126.4 59.7 %conditional.2 = (f32[192,1024]{0,1:T(8,128)S(1)}) conditional(s32[]{:T(128)} %convert_element_type.40, f32[192,1024]{0,1:T(8,128)S(1)} %get-tuple-element.193, (s32[]{:T(128)}, s32[]{:T(128)}, bf16[64,6144]{1,0:T(8,128)(2,1)S(1)}, bf16[16,192,1024]{1,2,0:T(8,128)(2,1)}, s32[]{:T(128)}, /*index=5*/f32[192,1024]{0,1:T(8,128)S(1)}) %tuple.36), branch_computations={%region_1.1_spmd, %region_2.2_spmd} | conditional | flops 75694088 | bytes 77020616 | solution.py:45
  131.4 13.3 %copy.17 = bf16[8,8,192,384]{3,1,2,0:T(8,128)(2,1)} copy(bf16[8,8,192,384]{3,2,1,0:T(8,128)(2,1)} %bitcast.18) | data formatting | bytes 18874368 | tf_op jit(solution)/shard_map/while/body/eval_jaxpr/cond
  154.6 25.7 %reshape.27 = bf16[64,192,383]{2,1,0:T(8,128)(2,1)} reshape(bf16[64,73536]{1,0:T(8,128)(2,1)} %slice.8) | data formatting | bytes 18825216 | tf_op jit(solution)/shard_map/while/body/eval_jaxpr/cond/branch_1_fun/reshape | solution.py:24
  187.4 59.7 %conditional.2 = (f32[192,1024]{0,1:T(8,128)S(1)}) conditional(s32[]{:T(128)} %convert_element_type.40, f32[192,1024]{0,1:T(8,128)S(1)} %get-tuple-element.193, (s32[]{:T(128)}, s32[]{:T(128)}, bf16[64,6144]{1,0:T(8,128)(2,1)S(1)}, bf16[16,192,1024]{1,2,0:T(8,128)(2,1)}, s32[]{:T(128)}, /*index=5*/f32[192,1024]{0,1:T(8,128)S(1)}) %tuple.36), branch_computations={%region_1.1_spmd, %region_2.2_spmd} | conditional | flops 75694088 | bytes 77020616 | solution.py:45
  192.4 13.3 %copy.17 = bf16[8,8,192,384]{3,1,2,0:T(8,128)(2,1)} copy(bf16[8,8,192,384]{3,2,1,0:T(8,128)(2,1)} %bitcast.18) | data formatting | bytes 18874368 | tf_op jit(solution)/shard_map/while/body/eval_jaxpr/cond
  215.5 25.7 %reshape.27 = bf16[64,192,383]{2,1,0:T(8,128)(2,1)} reshape(bf16[64,73536]{1,0:T(8,128)(2,1)} %slice.8) | data formatting | bytes 18825216 | tf_op jit(solution)/shard_map/while/body/eval_jaxpr/cond/branch_1_fun/reshape | solution.py:24
  248.3 59.7 %conditional.2 = (f32[192,1024]{0,1:T(8,128)S(1)}) conditional(s32[]{:T(128)} %convert_element_type.40, f32[192,1024]{0,1:T(8,128)S(1)} %get-tuple-element.193, (s32[]{:T(128)}, s32[]{:T(128)}, bf16[64,6144]{1,0:T(8,128)(2,1)S(1)}, bf16[16,192,1024]{1,2,0:T(8,128)(2,1)}, s32[]{:T(128)}, /*index=5*/f32[192,1024]{0,1:T(8,128)S(1)}) %tuple.36), branch_computations={%region_1.1_spmd, %region_2.2_spmd} | conditional | flops 75694088 | bytes 77020616 | solution.py:45
  253.3 13.3 %copy.17 = bf16[8,8,192,384]{3,1,2,0:T(8,128)(2,1)} copy(bf16[8,8,192,384]{3,2,1,0:T(8,128)(2,1)} %bitcast.18) | data formatting | bytes 18874368 | tf_op jit(solution)/shard_map/while/body/eval_jaxpr/cond
  276.4 25.7 %reshape.27 = bf16[64,192,383]{2,1,0:T(8,128)(2,1)} reshape(bf16[64,73536]{1,0:T(8,128)(2,1)} %slice.8) | data formatting | bytes 18825216 | tf_op jit(solution)/shard_map/while/body/eval_jaxpr/cond/branch_1_fun/reshape | solution.py:24
  309.2 59.7 %conditional.2 = (f32[192,1024]{0,1:T(8,128)S(1)}) conditional(s32[]{:T(128)} %convert_element_type.40, f32[192,1024]{0,1:T(8,128)S(1)} %get-tuple-element.193, (s32[]{:T(128)}, s32[]{:T(128)}, bf16[64,6144]{1,0:T(8,128)(2,1)S(1)}, bf16[16,192,1024]{1,2,0:T(8,128)(2,1)}, s32[]{:T(128)}, /*index=5*/f32[192,1024]{0,1:T(8,128)S(1)}) %tuple.36), branch_computations={%region_1.1_spmd, %region_2.2_spmd} | conditional | flops 75694088 | bytes 77020616 | solution.py:45
  314.2 13.3 %copy.17 = bf16[8,8,192,384]{3,1,2,0:T(8,128)(2,1)} copy(bf16[8,8,192,384]{3,2,1,0:T(8,128)(2,1)} %bitcast.18) | data formatting | bytes 18874368 | tf_op jit(solution)/shard_map/while/body/eval_jaxpr/cond
  337.4 25.7 %reshape.27 = bf16[64,192,383]{2,1,0:T(8,128)(2,1)} reshape(bf16[64,73536]{1,0:T(8,128)(2,1)} %slice.8) | data formatting | bytes 18825216 | tf_op jit(solution)/shard_map/while/body/eval_jaxpr/cond/branch_1_fun/reshape | solution.py:24
  370.2 59.7 %conditional.2 = (f32[192,1024]{0,1:T(8,128)S(1)}) conditional(s32[]{:T(128)} %convert_element_type.40, f32[192,1024]{0,1:T(8,128)S(1)} %get-tuple-element.193, (s32[]{:T(128)}, s32[]{:T(128)}, bf16[64,6144]{1,0:T(8,128)(2,1)S(1)}, bf16[16,192,1024]{1,2,0:T(8,128)(2,1)}, s32[]{:T(128)}, /*index=5*/f32[192,1024]{0,1:T(8,128)S(1)}) %tuple.36), branch_computations={%region_1.1_spmd, %region_2.2_spmd} | conditional | flops 75694088 | bytes 77020616 | solution.py:45
  398.3 25.7 %reshape.27 = bf16[64,192,383]{2,1,0:T(8,128)(2,1)} reshape(bf16[64,73536]{1,0:T(8,128)(2,1)} %slice.8) | data formatting | bytes 18825216 | tf_op jit(solution)/shard_map/while/body/eval_jaxpr/cond/branch_1_fun/reshape | solution.py:24
  431.1 59.7 %conditional.2 = (f32[192,1024]{0,1:T(8,128)S(1)}) conditional(s32[]{:T(128)} %convert_element_type.40, f32[192,1024]{0,1:T(8,128)S(1)} %get-tuple-element.193, (s32[]{:T(128)}, s32[]{:T(128)}, bf16[64,6144]{1,0:T(8,128)(2,1)S(1)}, bf16[16,192,1024]{1,2,0:T(8,128)(2,1)}, s32[]{:T(128)}, /*index=5*/f32[192,1024]{0,1:T(8,128)S(1)}) %tuple.36), branch_computations={%region_1.1_spmd, %region_2.2_spmd} | conditional | flops 75694088 | bytes 77020616 | solution.py:45
  436.1 13.3 %copy.17 = bf16[8,8,192,384]{3,1,2,0:T(8,128)(2,1)} copy(bf16[8,8,192,384]{3,2,1,0:T(8,128)(2,1)} %bitcast.18) | data formatting | bytes 18874368 | tf_op jit(solution)/shard_map/while/body/eval_jaxpr/cond
  459.2 25.7 %reshape.27 = bf16[64,192,383]{2,1,0:T(8,128)(2,1)} reshape(bf16[64,73536]{1,0:T(8,128)(2,1)} %slice.8) | data formatting | bytes 18825216 | tf_op jit(solution)/shard_map/while/body/eval_jaxpr/cond/branch_1_fun/reshape | solution.py:24
  492.0 59.7 %conditional.2 = (f32[192,1024]{0,1:T(8,128)S(1)}) conditional(s32[]{:T(128)} %convert_element_type.40, f32[192,1024]{0,1:T(8,128)S(1)} %get-tuple-element.193, (s32[]{:T(128)}, s32[]{:T(128)}, bf16[64,6144]{1,0:T(8,128)(2,1)S(1)}, bf16[16,192,1024]{1,2,0:T(8,128)(2,1)}, s32[]{:T(128)}, /*index=5*/f32[192,1024]{0,1:T(8,128)S(1)}) %tuple.36), branch_computations={%region_1.1_spmd, %region_2.2_spmd} | conditional | flops 75694088 | bytes 77020616 | solution.py:45
  497.0 13.3 %copy.17 = bf16[8,8,192,384]{3,1,2,0:T(8,128)(2,1)} copy(bf16[8,8,192,384]{3,2,1,0:T(8,128)(2,1)} %bitcast.18) | data formatting | bytes 18874368 | tf_op jit(solution)/shard_map/while/body/eval_jaxpr/cond
  520.2 25.7 %reshape.27 = bf16[64,192,383]{2,1,0:T(8,128)(2,1)} reshape(bf16[64,73536]{1,0:T(8,128)(2,1)} %slice.8) | data formatting | bytes 18825216 | tf_op jit(solution)/shard_map/while/body/eval_jaxpr/cond/branch_1_fun/reshape | solution.py:24
  552.9 59.7 %conditional.2 = (f32[192,1024]{0,1:T(8,128)S(1)}) conditional(s32[]{:T(128)} %convert_element_type.40, f32[192,1024]{0,1:T(8,128)S(1)} %get-tuple-element.193, (s32[]{:T(128)}, s32[]{:T(128)}, bf16[64,6144]{1,0:T(8,128)(2,1)S(1)}, bf16[16,192,1024]{1,2,0:T(8,128)(2,1)}, s32[]{:T(128)}, /*index=5*/f32[192,1024]{0,1:T(8,128)S(1)}) %tuple.36), branch_computations={%region_1.1_spmd, %region_2.2_spmd} | conditional | flops 75694088 | bytes 77020616 | solution.py:45
  557.9 13.3 %copy.17 = bf16[8,8,192,384]{3,1,2,0:T(8,128)(2,1)} copy(bf16[8,8,192,384]{3,2,1,0:T(8,128)(2,1)} %bitcast.18) | data formatting | bytes 18874368 | tf_op jit(solution)/shard_map/while/body/eval_jaxpr/cond
  581.1 25.7 %reshape.27 = bf16[64,192,383]{2,1,0:T(8,128)(2,1)} reshape(bf16[64,73536]{1,0:T(8,128)(2,1)} %slice.8) | data formatting | bytes 18825216 | tf_op jit(solution)/shard_map/while/body/eval_jaxpr/cond/branch_1_fun/reshape | solution.py:24
  613.9 59.7 %conditional.2 = (f32[192,1024]{0,1:T(8,128)S(1)}) conditional(s32[]{:T(128)} %convert_element_type.40, f32[192,1024]{0,1:T(8,128)S(1)} %get-tuple-element.193, (s32[]{:T(128)}, s32[]{:T(128)}, bf16[64,6144]{1,0:T(8,128)(2,1)S(1)}, bf16[16,192,1024]{1,2,0:T(8,128)(2,1)}, s32[]{:T(128)}, /*index=5*/f32[192,1024]{0,1:T(8,128)S(1)}) %tuple.36), branch_computations={%region_1.1_spmd, %region_2.2_spmd} | conditional | flops 75694088 | bytes 77020616 | solution.py:45
  642.0 25.7 %reshape.27 = bf16[64,192,383]{2,1,0:T(8,128)(2,1)} reshape(bf16[64,73536]{1,0:T(8,128)(2,1)} %slice.8) | data formatting | bytes 18825216 | tf_op jit(solution)/shard_map/while/body/eval_jaxpr/cond/branch_1_fun/reshape | solution.py:24
  674.8 59.7 %conditional.2 = (f32[192,1024]{0,1:T(8,128)S(1)}) conditional(s32[]{:T(128)} %convert_element_type.40, f32[192,1024]{0,1:T(8,128)S(1)} %get-tuple-element.193, (s32[]{:T(128)}, s32[]{:T(128)}, bf16[64,6144]{1,0:T(8,128)(2,1)S(1)}, bf16[16,192,1024]{1,2,0:T(8,128)(2,1)}, s32[]{:T(128)}, /*index=5*/f32[192,1024]{0,1:T(8,128)S(1)}) %tuple.36), branch_computations={%region_1.1_spmd, %region_2.2_spmd} | conditional | flops 75694088 | bytes 77020616 | solution.py:45
  679.8 13.3 %copy.17 = bf16[8,8,192,384]{3,1,2,0:T(8,128)(2,1)} copy(bf16[8,8,192,384]{3,2,1,0:T(8,128)(2,1)} %bitcast.18) | data formatting | bytes 18874368 | tf_op jit(solution)/shard_map/while/body/eval_jaxpr/cond
  702.9 25.7 %reshape.27 = bf16[64,192,383]{2,1,0:T(8,128)(2,1)} reshape(bf16[64,73536]{1,0:T(8,128)(2,1)} %slice.8) | data formatting | bytes 18825216 | tf_op jit(solution)/shard_map/while/body/eval_jaxpr/cond/branch_1_fun/reshape | solution.py:24
  735.7 59.7 %conditional.2 = (f32[192,1024]{0,1:T(8,128)S(1)}) conditional(s32[]{:T(128)} %convert_element_type.40, f32[192,1024]{0,1:T(8,128)S(1)} %get-tuple-element.193, (s32[]{:T(128)}, s32[]{:T(128)}, bf16[64,6144]{1,0:T(8,128)(2,1)S(1)}, bf16[16,192,1024]{1,2,0:T(8,128)(2,1)}, s32[]{:T(128)}, /*index=5*/f32[192,1024]{0,1:T(8,128)S(1)}) %tuple.36), branch_computations={%region_1.1_spmd, %region_2.2_spmd} | conditional | flops 75694088 | bytes 77020616 | solution.py:45
  740.7 13.3 %copy.17 = bf16[8,8,192,384]{3,1,2,0:T(8,128)(2,1)} copy(bf16[8,8,192,384]{3,2,1,0:T(8,128)(2,1)} %bitcast.18) | data formatting | bytes 18874368 | tf_op jit(solution)/shard_map/while/body/eval_jaxpr/cond
  763.9 25.7 %reshape.27 = bf16[64,192,383]{2,1,0:T(8,128)(2,1)} reshape(bf16[64,73536]{1,0:T(8,128)(2,1)} %slice.8) | data formatting | bytes 18825216 | tf_op jit(solution)/shard_map/while/body/eval_jaxpr/cond/branch_1_fun/reshape | solution.py:24
  796.7 59.7 %conditional.2 = (f32[192,1024]{0,1:T(8,128)S(1)}) conditional(s32[]{:T(128)} %convert_element_type.40, f32[192,1024]{0,1:T(8,128)S(1)} %get-tuple-element.193, (s32[]{:T(128)}, s32[]{:T(128)}, bf16[64,6144]{1,0:T(8,128)(2,1)S(1)}, bf16[16,192,1024]{1,2,0:T(8,128)(2,1)}, s32[]{:T(128)}, /*index=5*/f32[192,1024]{0,1:T(8,128)S(1)}) %tuple.36), branch_computations={%region_1.1_spmd, %region_2.2_spmd} | conditional | flops 75694088 | bytes 77020616 | solution.py:45
  801.6 13.3 %copy.17 = bf16[8,8,192,384]{3,1,2,0:T(8,128)(2,1)} copy(bf16[8,8,192,384]{3,2,1,0:T(8,128)(2,1)} %bitcast.18) | data formatting | bytes 18874368 | tf_op jit(solution)/shard_map/while/body/eval_jaxpr/cond
  824.8 25.7 %reshape.27 = bf16[64,192,383]{2,1,0:T(8,128)(2,1)} reshape(bf16[64,73536]{1,0:T(8,128)(2,1)} %slice.8) | data formatting | bytes 18825216 | tf_op jit(solution)/shard_map/while/body/eval_jaxpr/cond/branch_1_fun/reshape | solution.py:24
  857.6 59.7 %conditional.2 = (f32[192,1024]{0,1:T(8,128)S(1)}) conditional(s32[]{:T(128)} %convert_element_type.40, f32[192,1024]{0,1:T(8,128)S(1)} %get-tuple-element.193, (s32[]{:T(128)}, s32[]{:T(128)}, bf16[64,6144]{1,0:T(8,128)(2,1)S(1)}, bf16[16,192,1024]{1,2,0:T(8,128)(2,1)}, s32[]{:T(128)}, /*index=5*/f32[192,1024]{0,1:T(8,128)S(1)}) %tuple.36), branch_computations={%region_1.1_spmd, %region_2.2_spmd} | conditional | flops 75694088 | bytes 77020616 | solution.py:45
  885.7 25.7 %reshape.27 = bf16[64,192,383]{2,1,0:T(8,128)(2,1)} reshape(bf16[64,73536]{1,0:T(8,128)(2,1)} %slice.8) | data formatting | bytes 18825216 | tf_op jit(solution)/shard_map/while/body/eval_jaxpr/cond/branch_1_fun/reshape | solution.py:24
  918.5 59.7 %conditional.2 = (f32[192,1024]{0,1:T(8,128)S(1)}) conditional(s32[]{:T(128)} %convert_element_type.40, f32[192,1024]{0,1:T(8,128)S(1)} %get-tuple-element.193, (s32[]{:T(128)}, s32[]{:T(128)}, bf16[64,6144]{1,0:T(8,128)(2,1)S(1)}, bf16[16,192,1024]{1,2,0:T(8,128)(2,1)}, s32[]{:T(128)}, /*index=5*/f32[192,1024]{0,1:T(8,128)S(1)}) %tuple.36), branch_computations={%region_1.1_spmd, %region_2.2_spmd} | conditional | flops 75694088 | bytes 77020616 | solution.py:45
  923.5 13.3 %copy.17 = bf16[8,8,192,384]{3,1,2,0:T(8,128)(2,1)} copy(bf16[8,8,192,384]{3,2,1,0:T(8,128)(2,1)} %bitcast.18) | data formatting | bytes 18874368 | tf_op jit(solution)/shard_map/while/body/eval_jaxpr/cond
  946.7 25.7 %reshape.27 = bf16[64,192,383]{2,1,0:T(8,128)(2,1)} reshape(bf16[64,73536]{1,0:T(8,128)(2,1)} %slice.8) | data formatting | bytes 18825216 | tf_op jit(solution)/shard_map/while/body/eval_jaxpr/cond/branch_1_fun/reshape | solution.py:24
  979.4 59.7 %conditional.2 = (f32[192,1024]{0,1:T(8,128)S(1)}) conditional(s32[]{:T(128)} %convert_element_type.40, f32[192,1024]{0,1:T(8,128)S(1)} %get-tuple-element.193, (s32[]{:T(128)}, s32[]{:T(128)}, bf16[64,6144]{1,0:T(8,128)(2,1)S(1)}, bf16[16,192,1024]{1,2,0:T(8,128)(2,1)}, s32[]{:T(128)}, /*index=5*/f32[192,1024]{0,1:T(8,128)S(1)}) %tuple.36), branch_computations={%region_1.1_spmd, %region_2.2_spmd} | conditional | flops 75694088 | bytes 77020616 | solution.py:45
  984.4 13.3 %copy.17 = bf16[8,8,192,384]{3,1,2,0:T(8,128)(2,1)} copy(bf16[8,8,192,384]{3,2,1,0:T(8,128)(2,1)} %bitcast.18) | data formatting | bytes 18874368 | tf_op jit(solution)/shard_map/while/body/eval_jaxpr/cond
  1007.6 25.7 %reshape.27 = bf16[64,192,383]{2,1,0:T(8,128)(2,1)} reshape(bf16[64,73536]{1,0:T(8,128)(2,1)} %slice.8) | data formatting | bytes 18825216 | tf_op jit(solution)/shard_map/while/body/eval_jaxpr/cond/branch_1_fun/reshape | solution.py:24
  1040.3 28.8 %all_to_all.5 = bf16[8,192,1024]{2,1,0:T(8,128)(2,1)S(1)} all-to-all(bf16[8,192,1024]{2,1,0:T(8,128)(2,1)S(1)} %stack.2), channel_id=1, replica_groups=mesh['ctx'=16,'ch'=8] {'ch'}, dimensions={0} | all-to-all | bytes 6291456 | tf_op jit(solution)/shard_map/all_to_all | solution.py:10
  (183 shorter events, 398.2 us)
Async XLA Ops:
  6.5 46.6 %all-gather.2.cloned.1.call-start = ((), (), s32[]{:S(2)}) async-start(), calls=%async_computation.1 | async-start | bytes 6684672 | tf_op jit(solution)/shard_map/all_gather | solution.py:66
  64.2 975.4 %copy-start = (bf16[192,1024]{1,0:T(8,128)(2,1)S(1)}, bf16[192,1024]{1,0:T(8,128)(2,1)}, u32[]{:S(2)}) copy-start(bf16[192,1024]{1,0:T(8,128)(2,1)} %multiply_convert_fusion.1) | copy-start | bytes 1179652
  64.3 975.4 %copy-start.1 = (bf16[192,1024]{1,0:T(8,128)(2,1)S(1)}, bf16[192,1024]{1,0:T(8,128)(2,1)}, u32[]{:S(2)}) copy-start(bf16[192,1024]{1,0:T(8,128)(2,1)} %param.10) | copy-start | bytes 1179652
  64.3 975.4 %copy-start.2 = (f32[1024]{0:T(1024)S(1)}, f32[1024]{0:T(1024)}, u32[]{:S(2)}) copy-start(f32[1024]{0:T(1024)} %param.14) | copy-start | bytes 12292
  1039.7 29.8 %copy-start.3 = (bf16[8192,1024]{1,0:T(8,128)(2,1)S(1)}, bf16[8192,1024]{1,0:T(8,128)(2,1)}, u32[]{:S(2)}) copy-start(bf16[8192,1024]{1,0:T(8,128)(2,1)} %param.15) | copy-start | bytes 50331652
Sparse Core Ops, SparseCore 0:
  9.0 44.0 all-gather.1
